TPU v7x, 32 devices: a whole 2x2x4 slice. The times are simulated.
32 devices in a mesh: row: 8 (over y, x, core), col: 4 (over z).
Axes of the slice: x: 2, y: 2, z: 4, core: 2. Of those that a mesh axis runs over, the one named last changes fastest.
Arguments:
- rhs: float32 [32, 1024, 4096], P(None, 'row', 'col'), may hold values from -6 to 6
- factor: bfloat16 [32, 1024, 4, 1024], P(None, 'row', None, 'col'), may hold values from -0.09375 to 0.09375
- diag_inverse: bfloat16 [4, 1024, 1024], P(None, 'row'), may hold values from -1.5 to 1.5, as said below
Outputs:
- solution: float32 [4, 1024, 4096], P(None, 'row', 'col')
- remaining: float32 [28, 1024, 4096], P(None, 'row', 'col')
Inputs may be any that keep to these rules, and one draw needn't show every extreme that they name: Each diag_inverse[k] is lower triangular with diagonal entries from 0.5 to 1.5.
All inputs are finite; a program needn't handle non-finite values.
Results may differ from a plain program's by a relative error of at most 0.0044.
Values may be sent and summed in bfloat16 or wider, within the bound.
A program may use at most 192 MiB of HBM per device.

v0:
```python
import jax
import jax.numpy as jnp
from jax import lax
from jax.sharding import PartitionSpec as P

STEPS = 4


def shards(rhs, factor, diag_inverse):
    block_count, tile_rows, rhs_width = rhs.shape
    panel_cols = factor.shape[3]
    remaining_rows = rhs
    solved_list = []
    for section in range(STEPS):
        current = remaining_rows[0].astype(jnp.bfloat16)
        inverse_section = diag_inverse[section]
        own_rows = jnp.dot(
            inverse_section,
            lax.all_gather(current, "row", axis=0, tiled=True),
            preferred_element_type=jnp.float32,
        )
        whole_solved = lax.all_gather(own_rows.astype(jnp.bfloat16), "row", axis=0, tiled=True)
        solved_list.append(own_rows)
        later_count = block_count - section - 1
        lower_tiles = factor[section + 1 :, :, section, :]
        flat_tiles = lower_tiles.reshape(later_count * tile_rows, panel_cols)
        update = jnp.dot(
            lax.all_gather(flat_tiles, "col", axis=1, tiled=True),
            whole_solved,
            preferred_element_type=jnp.float32,
        )
        remaining_rows = remaining_rows[1:] - update.reshape(later_count, tile_rows, rhs_width)
    return (jnp.stack(solved_list), remaining_rows)


def solution(mesh):
    in_specs = (P(None, "row", "col"), P(None, "row", None, "col"), P(None, "row", None))
    out_specs = (P(None, "row", "col"), P(None, "row", "col"))
    return jax.shard_map(shards, mesh=mesh, in_specs=in_specs, out_specs=out_specs, check_vma=False)
```

profile of v0, /device:TPU:0, one launch (start us, length us, event | category | flops | bytes accessed | tf_op | source)
XLA Modules:
  0.0 999.3 jit_solution(11575915859656223268)
XLA Ops:
  9.1 32.0 %all-gather.33.cloned.1.call-done = bf16[1,1024,1024]{2,1,0:T(8,128)(2,1)} async-done(((bf16[1,128,1024]{2,1,0:T(8,128)(2,1)}), bf16[1,1024,1024]{2,1,0:T(8,128)(2,1)}) %all-gather.33.cloned.1.call-update) | async-done | bytes 2097168 | tf_op jit(solution)/shard_map/all_gather | solution.py:19
  44.0 8.8 slice.55
  52.8 3.9 copy.26
  56.8 15.2 %all-gather.17.cloned.1.call-done = bf16[1024,1024]{1,0:T(8,128)(2,1)} async-done(((bf16[128,1024]{1,0:T(8,128)(2,1)}), bf16[1024,1024]{1,0:T(8,128)(2,1)}) %all-gather.17.cloned.1.call-update) | async-done | bytes 2097168 | tf_op jit(solution)/shard_map/all_gather | solution.py:22
  72.0 147.0 %all-gather.19.cloned.1.call-done = bf16[3968,1024]{1,0:T(8,128)(2,1)} async-done(((bf16[3968,256]{1,0:T(8,128)(2,1)}), bf16[3968,1024]{1,0:T(8,128)(2,1)}) %all-gather.19.cloned.1.call-update) | async-done | bytes 8126480 | tf_op jit(solution)/shard_map/all_gather | solution.py:28
  219.0 15.9 %convolution_bitcast_fusion.3 = f32[3968,1024]{0,1:T(8,128)} fusion(bf16[1024,1024]{1,0:T(8,128)(2,1)} %all-gather.17.cloned.1.call-done, bf16[3968,1024]{1,0:T(8,128)(2,1)} %all-gather.19.cloned.1.call-done), kind=kOutput, calls=%fused_computation.7 | convolution fusion | flops 8321499136 | bytes 26476544 | tf_op jit(solution)/shard_map/dot_general | solution.py:27
  234.9 16.7 %copy.13 = f32[3968,1024]{1,0:T(8,128)} copy(f32[3968,1024]{0,1:T(8,128)} %convolution_bitcast_fusion.3) | data formatting | bytes 32505856 | tf_op jit(solution)/shard_map/dot_general | solution.py:27
  251.7 11.5 %slice_subtract_fusion = f32[31,128,1024]{2,1,0:T(8,128)S(1)} fusion(f32[31,128,1024]{2,1,0:T(8,128)} %bitcast.77, f32[32,128,1024]{2,1,0:T(8,128)} %param.3), kind=kLoop, calls=%fused_computation | loop fusion | flops 4063232 | bytes 48758784 | tf_op jit(solution)/shard_map/sub | solution.py:32
  263.2 5.6 copy-done
  270.0 10.0 %slice.59 = bf16[30,128,1,256]{3,2,1,0:T(2,128)(2,1)} slice(bf16[32,128,4,256]{3,2,1,0:T(4,128)(2,1)} %param.4), slice={[2:32], [0:128], [1:2], [0:256]} | slice | bytes 3932160 | tf_op jit(solution)/shard_map/slice | solution.py:25
  284.0 11.8 %all-gather.35.cloned.1.call-done = bf16[1,1024,1024]{2,1,0:T(8,128)(2,1)} async-done(((bf16[1,128,1024]{2,1,0:T(8,128)(2,1)}), bf16[1,1024,1024]{2,1,0:T(8,128)(2,1)}) %all-gather.35.cloned.1.call-update) | async-done | bytes 2097168 | tf_op jit(solution)/shard_map/all_gather | solution.py:19
  298.6 139.8 %all-gather.23.cloned.1.call-done = bf16[3840,1024]{1,0:T(8,128)(2,1)} async-done(((bf16[3840,256]{1,0:T(8,128)(2,1)}), bf16[3840,1024]{1,0:T(8,128)(2,1)}) %all-gather.23.cloned.1.call-update) | async-done | bytes 7864336 | tf_op jit(solution)/shard_map/all_gather | solution.py:28
  438.3 28.4 %all-gather.21.cloned.1.call-done = bf16[1024,1024]{1,0:T(8,128)(2,1)} async-done(((bf16[128,1024]{1,0:T(8,128)(2,1)}), bf16[1024,1024]{1,0:T(8,128)(2,1)}) %all-gather.21.cloned.1.call-update) | async-done | bytes 2097168 | tf_op jit(solution)/shard_map/all_gather | solution.py:22
  466.8 15.3 %convolution_bitcast_fusion.2 = f32[3840,1024]{0,1:T(8,128)} fusion(bf16[1024,1024]{1,0:T(8,128)(2,1)} %all-gather.21.cloned.1.call-done, bf16[3840,1024]{1,0:T(8,128)(2,1)} %all-gather.23.cloned.1.call-done), kind=kOutput, calls=%fused_computation.6 | convolution fusion | flops 8053063680 | bytes 25690112 | tf_op jit(solution)/shard_map/dot_general | solution.py:27
  482.1 15.7 %copy.16 = f32[3840,1024]{1,0:T(8,128)} copy(f32[3840,1024]{0,1:T(8,128)} %convolution_bitcast_fusion.2) | data formatting | bytes 31457280 | tf_op jit(solution)/shard_map/dot_general | solution.py:27
  497.8 11.2 %slice_subtract_fusion.1 = f32[30,128,1024]{2,1,0:T(8,128)S(1)} fusion(f32[30,128,1024]{2,1,0:T(8,128)} %bitcast.78, f32[31,128,1024]{2,1,0:T(8,128)} %copy-done), kind=kLoop, calls=%fused_computation.1 | loop fusion | flops 3932160 | bytes 47185920 | tf_op jit(solution)/shard_map/sub | solution.py:32
  508.9 5.4 copy-done.1
  515.3 9.6 slice.63
  528.8 14.4 %all-gather.37.cloned.1.call-done = bf16[1,1024,1024]{2,1,0:T(8,128)(2,1)} async-done(((bf16[1,128,1024]{2,1,0:T(8,128)(2,1)}), bf16[1,1024,1024]{2,1,0:T(8,128)(2,1)}) %all-gather.37.cloned.1.call-update) | async-done | bytes 2097168 | tf_op jit(solution)/shard_map/all_gather | solution.py:19
  546.1 135.5 %all-gather.27.cloned.1.call-done = bf16[3712,1024]{1,0:T(8,128)(2,1)} async-done(((bf16[3712,256]{1,0:T(8,128)(2,1)}), bf16[3712,1024]{1,0:T(8,128)(2,1)}) %all-gather.27.cloned.1.call-update) | async-done | bytes 7602192 | tf_op jit(solution)/shard_map/all_gather | solution.py:28
  681.6 28.6 %all-gather.25.cloned.1.call-done = bf16[1024,1024]{1,0:T(8,128)(2,1)} async-done(((bf16[128,1024]{1,0:T(8,128)(2,1)}), bf16[1024,1024]{1,0:T(8,128)(2,1)}) %all-gather.25.cloned.1.call-update) | async-done | bytes 2097168 | tf_op jit(solution)/shard_map/all_gather | solution.py:22
  710.2 15.1 %convolution_bitcast_fusion.1 = f32[3712,1024]{0,1:T(8,128)} fusion(bf16[1024,1024]{1,0:T(8,128)(2,1)} %all-gather.25.cloned.1.call-done, bf16[3712,1024]{1,0:T(8,128)(2,1)} %all-gather.27.cloned.1.call-done), kind=kOutput, calls=%fused_computation.5 | convolution fusion | flops 7784628224 | bytes 24903680 | tf_op jit(solution)/shard_map/dot_general | solution.py:27
  725.3 15.5 %copy.19 = f32[3712,1024]{1,0:T(8,128)} copy(f32[3712,1024]{0,1:T(8,128)} %convolution_bitcast_fusion.1) | data formatting | bytes 30408704 | tf_op jit(solution)/shard_map/dot_general | solution.py:27
  740.8 10.8 %slice_subtract_fusion.2 = f32[29,128,1024]{2,1,0:T(8,128)S(1)} fusion(f32[29,128,1024]{2,1,0:T(8,128)} %bitcast.79, f32[30,128,1024]{2,1,0:T(8,128)} %copy-done.1), kind=kLoop, calls=%fused_computation.2 | loop fusion | flops 3801088 | bytes 45613056 | tf_op jit(solution)/shard_map/sub | solution.py:32
  751.7 5.3 copy-done.2
  758.0 7.5 slice.67
  767.2 18.6 %all-gather.39.cloned.1.call-done = bf16[1,1024,1024]{2,1,0:T(8,128)(2,1)} async-done(((bf16[1,128,1024]{2,1,0:T(8,128)(2,1)}), bf16[1,1024,1024]{2,1,0:T(8,128)(2,1)}) %all-gather.39.cloned.1.call-update) | async-done | bytes 2097168 | tf_op jit(solution)/shard_map/all_gather | solution.py:19
  791.3 128.7 %all-gather.31.cloned.1.call-done = bf16[3584,1024]{1,0:T(8,128)(2,1)} async-done(((bf16[3584,256]{1,0:T(8,128)(2,1)}), bf16[3584,1024]{1,0:T(8,128)(2,1)}) %all-gather.31.cloned.1.call-update) | async-done | bytes 7340048 | tf_op jit(solution)/shard_map/all_gather | solution.py:28
  920.0 27.9 %all-gather.29.cloned.1.call-done = bf16[1024,1024]{1,0:T(8,128)(2,1)} async-done(((bf16[128,1024]{1,0:T(8,128)(2,1)}), bf16[1024,1024]{1,0:T(8,128)(2,1)}) %all-gather.29.cloned.1.call-update) | async-done | bytes 2097168 | tf_op jit(solution)/shard_map/all_gather | solution.py:22
  947.8 13.8 %convolution_bitcast_fusion = f32[3584,1024]{0,1:T(8,128)} fusion(bf16[1024,1024]{1,0:T(8,128)(2,1)} %all-gather.29.cloned.1.call-done, bf16[3584,1024]{1,0:T(8,128)(2,1)} %all-gather.31.cloned.1.call-done), kind=kOutput, calls=%fused_computation.4 | convolution fusion | flops 7516192768 | bytes 24117248 | tf_op jit(solution)/shard_map/dot_general | solution.py:27
  961.6 15.4 %copy.22 = f32[3584,1024]{1,0:T(8,128)} copy(f32[3584,1024]{0,1:T(8,128)} %convolution_bitcast_fusion) | data formatting | bytes 29360128 | tf_op jit(solution)/shard_map/dot_general | solution.py:27
  977.0 15.2 %slice_subtract_fusion.3 = f32[28,128,1024]{2,1,0:T(8,128)} fusion(f32[28,128,1024]{2,1,0:T(8,128)} %bitcast.80, f32[29,128,1024]{2,1,0:T(8,128)} %copy-done.2), kind=kLoop, calls=%fused_computation.3 | loop fusion | flops 3670016 | bytes 44040192 | tf_op jit(solution)/shard_map/sub | solution.py:32
  (41 shorter events, 28.8 us)
Async XLA Ops:
  7.2 33.9 %all-gather.33.cloned.1.call-start = ((), (), s32[]{:S(2)}) async-start(), calls=%async_computation.8 | async-start | bytes 2359296 | tf_op jit(solution)/shard_map/all_gather | solution.py:19
  9.0 63.0 %all-gather.17.cloned.1.call-start = ((), (), s32[]{:S(2)}) async-start(), calls=%async_computation | async-start | bytes 2359296 | tf_op jit(solution)/shard_map/all_gather | solution.py:22
  44.0 175.1 %all-gather.19.cloned.1.call-start = ((), (), s32[]{:S(2)}) async-start(), calls=%async_computation.1 | async-start | bytes 10158080 | tf_op jit(solution)/shard_map/all_gather | solution.py:28
  56.8 239.0 %all-gather.35.cloned.1.call-start = ((), (), s32[]{:S(2)}) async-start(), calls=%async_computation.9 | async-start | bytes 2359296 | tf_op jit(solution)/shard_map/all_gather | solution.py:19
  263.2 5.6 copy-start
  269.5 26.2 %copy-start.3 = (bf16[4,128,1024]{2,1,0:T(8,128)(2,1)S(1)}, bf16[4,128,1024]{2,1,0:T(8,128)(2,1)}, u32[]{:S(2)}) copy-start(bf16[4,128,1024]{2,1,0:T(8,128)(2,1)} %param.5) | copy-start | bytes 3145732
  269.5 168.8 %all-gather.23.cloned.1.call-start = ((), (), s32[]{:S(2)}) async-start(), calls=%async_computation.3 | async-start | bytes 9830400 | tf_op jit(solution)/shard_map/all_gather | solution.py:28
  283.9 182.8 %all-gather.21.cloned.1.call-start = ((), (), s32[]{:S(2)}) async-start(), calls=%async_computation.2 | async-start | bytes 2359296 | tf_op jit(solution)/shard_map/all_gather | solution.py:22
  298.5 244.6 %all-gather.37.cloned.1.call-start = ((), (), s32[]{:S(2)}) async-start(), calls=%async_computation.10 | async-start | bytes 2359296 | tf_op jit(solution)/shard_map/all_gather | solution.py:19
  508.9 5.4 copy-start.1
  515.1 166.5 %all-gather.27.cloned.1.call-start = ((), (), s32[]{:S(2)}) async-start(), calls=%async_computation.5 | async-start | bytes 9502720 | tf_op jit(solution)/shard_map/all_gather | solution.py:28
  528.7 181.5 %all-gather.25.cloned.1.call-start = ((), (), s32[]{:S(2)}) async-start(), calls=%async_computation.4 | async-start | bytes 2359296 | tf_op jit(solution)/shard_map/all_gather | solution.py:22
  546.1 239.7 %all-gather.39.cloned.1.call-start = ((), (), s32[]{:S(2)}) async-start(), calls=%async_computation.11 | async-start | bytes 2359296 | tf_op jit(solution)/shard_map/all_gather | solution.py:19
  751.6 5.3 copy-start.2
  757.7 162.2 %all-gather.31.cloned.1.call-start = ((), (), s32[]{:S(2)}) async-start(), calls=%async_computation.7 | async-start | bytes 9175040 | tf_op jit(solution)/shard_map/all_gather | solution.py:28
  767.2 180.6 %all-gather.29.cloned.1.call-start = ((), (), s32[]{:S(2)}) async-start(), calls=%async_computation.6 | async-start | bytes 2359296 | tf_op jit(solution)/shard_map/all_gather | solution.py:22
Sparse Core Ops, SparseCore 0:
  10.5 30.5 all-gather.32
  44.1 27.8 all-gather.16
  74.1 144.8 all-gather.18
  269.6 26.0 all-gather.34
  297.7 140.5 all-gather.22
  440.6 26.0 all-gather.20
  515.2 27.8 all-gather.36
  545.3 136.2 all-gather.26
  684.1 26.0 all-gather.24
  757.9 27.8 all-gather.38
  787.9 131.9 all-gather.30
  921.7 26.0 all-gather.28
where the time goes:
time: 1010 us; the launch traced here: 999 us
  waiting for transfers between devices  728 us (72%)
  local copies, waits for them, and re-layouts  133 us (13%)
  matrix products  71.6 us (7%)
  other arithmetic  51.3 us (5%)
  between operations  14.5 us (1%)
    all_gather x4, waiting for transfers between devices, shards(): lax.all_gather(flat_tiles, 'col', axis=1, tiled=True)  551 us
    all_gather x4, waiting for transfers between devices, shards(): lax.all_gather(own_rows.astype(jnp.bfloat16), 'row', axis=0, tiled=True)  100 us
    all_gather x4, waiting for transfers between devices, shards(): lax.all_gather(current, 'row', axis=0, tiled=True)  76.7 us
    dot_general x4, local copies, waits for them, and re-layouts, shards(): jnp.dot(lax.all_gather(flat_tiles, 'col', axis=1, tiled=True), whole_solv...  63.3 us
    dot_general x4, matrix products, shards(): jnp.dot(lax.all_gather(flat_tiles, 'col', axis=1, tiled=True), whole_solv...  60.2 us
    sub x4, other arithmetic, shards(): remaining_rows[1:] - update.reshape(later_count, tile_rows, rhs_width)  48.7 us
    slice x4, local copies, waits for them, and re-layouts, shards(): lower_tiles = factor[section + 1:, :, section, :]  35.8 us
    unnamed x12, local copies, waits for them, and re-layouts  29.6 us
  transfers between devices with their start and end apart: 12, of which 12 were waited for; matrix products, arithmetic and copies ran while one was open for 6% of the time, Pallas kernels for 0%

commit v1 on v0

--- a/solution.py
+++ b/solution.py
@@ -14,10 +14,40 @@
     for section in range(STEPS):
         current = remaining_rows[0].astype(jnp.bfloat16)
         inverse_section = diag_inverse[section]
+
+        def _launch_vector(x_part, device_axis, array_axis):
+            arr_now = lax.axis_size(device_axis)
+            formed = lax.axis_index(device_axis)
+            t1, b_now, step_out = (arr_now, formed, x_part.shape[array_axis])
+            k_now = range(t1)
+            y = map(lambda p: (p, (p + 1) % t1), k_now)
+            samples = list(y)
+            taken_in = range(t1)
+            piece_out = map(lambda p: (p, (p - 1) % t1), taken_in)
+            column = list(piece_out)
+            spare = jnp.zeros(
+                (*x_part.shape[:array_axis], t1 * step_out, *x_part.shape[array_axis + 1 :]),
+                x_part.dtype,
+            )
+            spare = lax.dynamic_update_slice_in_dim(
+                spare, x_part, b_now * step_out, axis=array_axis
+            )
+            extra = block_out = x_part
+            near = t1 // 2
+            for j in range(1, near + 1):
+                extra = lax.ppermute(extra, device_axis, samples)
+                spare = lax.dynamic_update_slice_in_dim(
+                    spare, extra, (b_now - j) % t1 * step_out, axis=array_axis
+                )
+                if j < t1 - near:
+                    block_out = lax.ppermute(block_out, device_axis, column)
+                    spare = lax.dynamic_update_slice_in_dim(
+                        spare, block_out, (b_now + j) % t1 * step_out, axis=array_axis
+                    )
+            return spare
+
         own_rows = jnp.dot(
-            inverse_section,
-            lax.all_gather(current, "row", axis=0, tiled=True),
-            preferred_element_type=jnp.float32,
+            inverse_section, _launch_vector(current, "row", 0), preferred_element_type=jnp.float32
         )
         whole_solved = lax.all_gather(own_rows.astype(jnp.bfloat16), "row", axis=0, tiled=True)
         solved_list.append(own_rows)

time: 1010 us -> 779 us (0.77)
  waiting for transfers between devices: 728 us -> 468 us
  starting transfers between devices: 1.35 us -> 35.8 us
    all_gather x4, waiting for transfers between devices: 551 us -> 284 us  [shards(): lax.all_gather(flat_tiles, 'col', axis=1, tiled=True)]
    ppermute x0 -> x28, waiting for transfers between devices: none -> 92.2 us  [the longest x16 88 us: _launch_vector(): extra = lax.ppermute(extra, device_axis, samples)]
    all_gather x4 -> x0, waiting for transfers between devices: 76.7 us -> none  [shards(): lax.all_gather(current, 'row', axis=0, tiled=True)]
    ppermute x0 -> x28, starting transfers between devices: none -> 34.6 us  [the longest x12 32.4 us: _launch_vector(): block_out = lax.ppermute(block_out, device_axis, column)]
    unnamed x12 -> x13, local copies, waits for them, and re-layouts: 29.6 us -> 30.5 us
  transfers between devices with their start and end apart: 12 -> 36, of which waited for: 12 -> 27; matrix products, arithmetic and copies ran while one was open for 6% -> 24% of each run, Pallas kernels for 0% -> 0%
where the time goes in v1:
time: 779 us; the launch traced here: 770 us
  waiting for transfers between devices  468 us (60%)
  local copies, waits for them, and re-layouts  133 us (17%)
  matrix products  68.1 us (9%)
  other arithmetic  50.6 us (6%)
  starting transfers between devices  35.8 us (5%)
  between operations  14.8 us (2%)
    all_gather x4, waiting for transfers between devices, shards(): lax.all_gather(flat_tiles, 'col', axis=1, tiled=True)  284 us
    all_gather x4, waiting for transfers between devices, shards(): lax.all_gather(own_rows.astype(jnp.bfloat16), 'row', axis=0, tiled=True)  92.1 us
    ppermute x16, waiting for transfers between devices, _launch_vector(): extra = lax.ppermute(extra, device_axis, samples)  88 us
    dot_general x4, local copies, waits for them, and re-layouts, shards(): jnp.dot(lax.all_gather(flat_tiles, 'col', axis=1, tiled=True), whole_solv...  63.5 us
    dot_general x4, matrix products, shards(): jnp.dot(lax.all_gather(flat_tiles, 'col', axis=1, tiled=True), whole_solv...  60 us
    sub x4, other arithmetic, shards(): remaining_rows[1:] - update.reshape(later_count, tile_rows, rhs_width)  49.3 us
    slice x4, local copies, waits for them, and re-layouts, shards(): lower_tiles = factor[section + 1:, :, section, :]  36.2 us
    ppermute x12, starting transfers between devices, _launch_vector(): block_out = lax.ppermute(block_out, device_axis, column)  32.4 us
  transfers between devices with their start and end apart: 36, of which 27 were waited for; matrix products, arithmetic and copies ran while one was open for 24% of the time, Pallas kernels for 0%

profile of v1, /device:TPU:0, one launch (start us, length us, event | category | flops | bytes accessed | tf_op | source)
XLA Modules:
  0.0 770.3 jit_solution(4459046066774030571)
XLA Ops:
  39.6 8.8 %slice.55 = bf16[31,128,1,256]{3,2,1,0:T(2,128)(2,1)} slice(bf16[32,128,4,256]{3,2,1,0:T(4,128)(2,1)} %param.4), slice={[1:32], [0:128], [0:1], [0:256]} | slice | bytes 4063232 | tf_op jit(solution)/shard_map/slice | solution.py:55
  52.4 10.2 %slice.59 = bf16[30,128,1,256]{3,2,1,0:T(2,128)(2,1)} slice(bf16[32,128,4,256]{3,2,1,0:T(4,128)(2,1)} %param.4), slice={[2:32], [0:128], [1:2], [0:256]} | slice | bytes 3932160 | tf_op jit(solution)/shard_map/slice | solution.py:55
  67.0 7.5 all-gather.9.cloned.1.call-done
  74.5 147.0 %all-gather.11.cloned.1.call-done = bf16[3968,1024]{1,0:T(8,128)(2,1)} async-done(((bf16[3968,256]{1,0:T(8,128)(2,1)}), bf16[3968,1024]{1,0:T(8,128)(2,1)}) %all-gather.11.cloned.1.call-update) | async-done | bytes 8126480 | tf_op jit(solution)/shard_map/all_gather | solution.py:58
  221.5 15.9 %convolution_bitcast_fusion.3 = f32[3968,1024]{0,1:T(8,128)} fusion(bf16[1024,1024]{0,1:T(8,128)(2,1)} %all-gather.9.cloned.1.call-done, bf16[3968,1024]{1,0:T(8,128)(2,1)} %all-gather.11.cloned.1.call-done), kind=kOutput, calls=%fused_computation.7 | convolution fusion | flops 8321499136 | bytes 26476544 | tf_op jit(solution)/shard_map/dot_general | solution.py:57
  237.4 16.8 %copy.11 = f32[3968,1024]{1,0:T(8,128)} copy(f32[3968,1024]{0,1:T(8,128)} %convolution_bitcast_fusion.3) | data formatting | bytes 32505856 | tf_op jit(solution)/shard_map/dot_general | solution.py:57
  254.2 11.8 %slice_subtract_fusion = f32[31,128,1024]{2,1,0:T(8,128)S(1)} fusion(f32[31,128,1024]{2,1,0:T(8,128)} %bitcast.76, f32[32,128,1024]{2,1,0:T(8,128)} %param.3), kind=kLoop, calls=%fused_computation | loop fusion | flops 4063232 | bytes 48758784 | tf_op jit(solution)/shard_map/sub | solution.py:62
  296.1 6.6 collective-permute-done.13
  304.3 9.6 %slice.63 = bf16[29,128,1,256]{3,2,1,0:T(2,128)(2,1)} slice(bf16[32,128,4,256]{3,2,1,0:T(4,128)(2,1)} %param.4), slice={[3:32], [0:128], [2:3], [0:256]} | slice | bytes 3801088 | tf_op jit(solution)/shard_map/slice | solution.py:55
  317.9 43.9 %all-gather.15.cloned.1.call-done = bf16[3840,1024]{1,0:T(8,128)(2,1)} async-done(((bf16[3840,256]{1,0:T(8,128)(2,1)}), bf16[3840,1024]{1,0:T(8,128)(2,1)}) %all-gather.15.cloned.1.call-update) | async-done | bytes 7864336 | tf_op jit(solution)/shard_map/all_gather | solution.py:58
  361.9 28.1 %all-gather.13.cloned.1.call-done = bf16[1024,1024]{0,1:T(8,128)(2,1)} async-done(((bf16[128,1024]{0,1:T(8,128)(2,1)}), bf16[1024,1024]{0,1:T(8,128)(2,1)}) %all-gather.13.cloned.1.call-update) | async-done | bytes 2097168 | tf_op jit(solution)/shard_map/all_gather | solution.py:52
  390.0 15.2 %convolution_bitcast_fusion.2 = f32[3840,1024]{0,1:T(8,128)} fusion(bf16[1024,1024]{0,1:T(8,128)(2,1)} %all-gather.13.cloned.1.call-done, bf16[3840,1024]{1,0:T(8,128)(2,1)} %all-gather.15.cloned.1.call-done), kind=kOutput, calls=%fused_computation.6 | convolution fusion | flops 8053063680 | bytes 25690112 | tf_op jit(solution)/shard_map/dot_general | solution.py:57
  405.3 15.7 %copy.13 = f32[3840,1024]{1,0:T(8,128)} copy(f32[3840,1024]{0,1:T(8,128)} %convolution_bitcast_fusion.2) | data formatting | bytes 31457280 | tf_op jit(solution)/shard_map/dot_general | solution.py:57
  421.0 11.3 %slice_subtract_fusion.1 = f32[30,128,1024]{2,1,0:T(8,128)S(1)} fusion(f32[30,128,1024]{2,1,0:T(8,128)} %bitcast.77, f32[31,128,1024]{2,1,0:T(8,128)} %copy-done), kind=kLoop, calls=%fused_computation.1 | loop fusion | flops 3932160 | bytes 47185920 | tf_op jit(solution)/shard_map/sub | solution.py:62
  449.2 6.5 collective-permute-done.16
  458.5 6.5 collective-permute-done.18
  465.1 6.6 collective-permute-done.20
  473.5 7.5 slice.67
  483.0 45.3 %all-gather.19.cloned.1.call-done = bf16[3712,1024]{1,0:T(8,128)(2,1)} async-done(((bf16[3712,256]{1,0:T(8,128)(2,1)}), bf16[3712,1024]{1,0:T(8,128)(2,1)}) %all-gather.19.cloned.1.call-update) | async-done | bytes 7602192 | tf_op jit(solution)/shard_map/all_gather | solution.py:58
  528.3 28.1 %all-gather.17.cloned.1.call-done = bf16[1024,1024]{0,1:T(8,128)(2,1)} async-done(((bf16[128,1024]{0,1:T(8,128)(2,1)}), bf16[1024,1024]{0,1:T(8,128)(2,1)}) %all-gather.17.cloned.1.call-update) | async-done | bytes 2097168 | tf_op jit(solution)/shard_map/all_gather | solution.py:52
  556.5 15.1 %convolution_bitcast_fusion.1 = f32[3712,1024]{0,1:T(8,128)} fusion(bf16[1024,1024]{0,1:T(8,128)(2,1)} %all-gather.17.cloned.1.call-done, bf16[3712,1024]{1,0:T(8,128)(2,1)} %all-gather.19.cloned.1.call-done), kind=kOutput, calls=%fused_computation.5 | convolution fusion | flops 7784628224 | bytes 24903680 | tf_op jit(solution)/shard_map/dot_general | solution.py:57
  571.6 15.6 %copy.15 = f32[3712,1024]{1,0:T(8,128)} copy(f32[3712,1024]{0,1:T(8,128)} %convolution_bitcast_fusion.1) | data formatting | bytes 30408704 | tf_op jit(solution)/shard_map/dot_general | solution.py:57
  587.2 11.0 %slice_subtract_fusion.2 = f32[29,128,1024]{2,1,0:T(8,128)S(1)} fusion(f32[29,128,1024]{2,1,0:T(8,128)} %bitcast.78, f32[30,128,1024]{2,1,0:T(8,128)} %copy-done.1), kind=kLoop, calls=%fused_computation.2 | loop fusion | flops 3801088 | bytes 45613056 | tf_op jit(solution)/shard_map/sub | solution.py:62
  606.3 6.1 collective-permute-done.21
  615.0 6.5 collective-permute-done.23
  624.3 6.5 collective-permute-done.25
  631.0 6.6 collective-permute-done.27
  643.3 47.3 %all-gather.23.cloned.1.call-done = bf16[3584,1024]{1,0:T(8,128)(2,1)} async-done(((bf16[3584,256]{1,0:T(8,128)(2,1)}), bf16[3584,1024]{1,0:T(8,128)(2,1)}) %all-gather.23.cloned.1.call-update) | async-done | bytes 7340048 | tf_op jit(solution)/shard_map/all_gather | solution.py:58
  690.6 28.3 %all-gather.21.cloned.1.call-done = bf16[1024,1024]{0,1:T(8,128)(2,1)} async-done(((bf16[128,1024]{0,1:T(8,128)(2,1)}), bf16[1024,1024]{0,1:T(8,128)(2,1)}) %all-gather.21.cloned.1.call-update) | async-done | bytes 2097168 | tf_op jit(solution)/shard_map/all_gather | solution.py:52
  718.9 13.8 %convolution_bitcast_fusion = f32[3584,1024]{0,1:T(8,128)} fusion(bf16[1024,1024]{0,1:T(8,128)(2,1)} %all-gather.21.cloned.1.call-done, bf16[3584,1024]{1,0:T(8,128)(2,1)} %all-gather.23.cloned.1.call-done), kind=kOutput, calls=%fused_computation.4 | convolution fusion | flops 7516192768 | bytes 24117248 | tf_op jit(solution)/shard_map/dot_general | solution.py:57
  732.7 15.4 %copy.17 = f32[3584,1024]{1,0:T(8,128)} copy(f32[3584,1024]{0,1:T(8,128)} %convolution_bitcast_fusion) | data formatting | bytes 29360128 | tf_op jit(solution)/shard_map/dot_general | solution.py:57
  748.1 15.2 %slice_subtract_fusion.3 = f32[28,128,1024]{2,1,0:T(8,128)} fusion(f32[28,128,1024]{2,1,0:T(8,128)} %bitcast.79, f32[29,128,1024]{2,1,0:T(8,128)} %copy-done.2), kind=kLoop, calls=%fused_computation.3 | loop fusion | flops 3670016 | bytes 44040192 | tf_op jit(solution)/shard_map/sub | solution.py:62
  (118 shorter events, 119.0 us)
Async XLA Ops:
  7.2 67.4 %all-gather.9.cloned.1.call-start = ((), (), s32[]{:S(2)}) async-start(), calls=%async_computation | async-start | bytes 2359296 | tf_op jit(solution)/shard_map/all_gather | solution.py:52
  8.6 7.6 collective-permute-start
  9.1 8.6 %collective-permute-start.1 = (bf16[128,1024]{1,0:T(8,128)(2,1)S(1)}, bf16[128,1024]{1,0:T(8,128)(2,1)S(1)}, u32[]{:S(2)}, u32[]{:S(2)}) collective-permute-start(bf16[128,1024]{1,0:T(8,128)(2,1)S(1)} %get-tuple-element.13), channel_id=1, source_target_pairs={{0,28},{4,0},{8,4},{12,8},{16,12},{20,16},{24,20},{28,24},{1,29},{... | collective-permute-start | bytes 786440 | tf_op jit(solution)/shard_map/ppermute | solution.py:43
  16.2 6.9 collective-permute-start.2
  17.7 7.6 collective-permute-start.3
  23.0 7.4 collective-permute-start.4
  30.5 6.7 collective-permute-start.6
  39.6 181.9 %all-gather.11.cloned.1.call-start = ((), (), s32[]{:S(2)}) async-start(), calls=%async_computation.1 | async-start | bytes 10158080 | tf_op jit(solution)/shard_map/all_gather | solution.py:58
  52.4 309.5 %all-gather.15.cloned.1.call-start = ((), (), s32[]{:S(2)}) async-start(), calls=%async_computation.3 | async-start | bytes 9830400 | tf_op jit(solution)/shard_map/all_gather | solution.py:58
  66.5 323.5 %all-gather.13.cloned.1.call-start = ((), (), s32[]{:S(2)}) async-start(), calls=%async_computation.2 | async-start | bytes 2359296 | tf_op jit(solution)/shard_map/all_gather | solution.py:52
  271.6 7.7 %collective-permute-start.7 = (bf16[128,1024]{1,0:T(8,128)(2,1)S(1)}, bf16[128,1024]{1,0:T(8,128)(2,1)S(1)}, u32[]{:S(2)}, u32[]{:S(2)}) collective-permute-start(bf16[128,1024]{1,0:T(8,128)(2,1)S(1)} %get-tuple-element.11), channel_id=1, source_target_pairs={{0,4},{4,8},{8,12},{12,16},{16,20},{20,24},{24,28},{28,0},{1,5},{5... | collective-permute-start | bytes 786440 | tf_op jit(solution)/shard_map/ppermute | solution.py:38
  271.7 7.6 collective-permute-start.8
  279.3 8.1 %collective-permute-start.9 = (bf16[128,1024]{1,0:T(8,128)(2,1)S(1)}, bf16[128,1024]{1,0:T(8,128)(2,1)S(1)}, u32[]{:S(2)}, u32[]{:S(2)}) collective-permute-start(bf16[128,1024]{1,0:T(8,128)(2,1)S(1)} %collective-permute-done.7), channel_id=1, source_target_pairs={{0,4},{4,8},{8,12},{12,16},{16,20},{20,24},{24,28},{28,0},{1,5},{5... | collective-permute-start | bytes 786440 | tf_op jit(solution)/shard_map/ppermute | solution.py:38
  279.3 8.2 %collective-permute-start.10 = (bf16[128,1024]{1,0:T(8,128)(2,1)S(1)}, bf16[128,1024]{1,0:T(8,128)(2,1)S(1)}, u32[]{:S(2)}, u32[]{:S(2)}) collective-permute-start(bf16[128,1024]{1,0:T(8,128)(2,1)S(1)} %collective-permute-done.8), channel_id=1, source_target_pairs={{0,28},{4,0},{8,4},{12,8},{16,12},{20,16},{24,20},{28,24},{1,29},{... | collective-permute-start | bytes 786440 | tf_op jit(solution)/shard_map/ppermute | solution.py:43
  287.4 8.6 %collective-permute-start.11 = (bf16[128,1024]{1,0:T(8,128)(2,1)S(1)}, bf16[128,1024]{1,0:T(8,128)(2,1)S(1)}, u32[]{:S(2)}, u32[]{:S(2)}) collective-permute-start(bf16[128,1024]{1,0:T(8,128)(2,1)S(1)} %collective-permute-done.9), channel_id=1, source_target_pairs={{0,4},{4,8},{8,12},{12,16},{16,20},{20,24},{24,28},{28,0},{1,5},{5... | collective-permute-start | bytes 786440 | tf_op jit(solution)/shard_map/ppermute | solution.py:38
  287.5 8.6 %collective-permute-start.12 = (bf16[128,1024]{1,0:T(8,128)(2,1)S(1)}, bf16[128,1024]{1,0:T(8,128)(2,1)S(1)}, u32[]{:S(2)}, u32[]{:S(2)}) collective-permute-start(bf16[128,1024]{1,0:T(8,128)(2,1)S(1)} %collective-permute-done.10), channel_id=1, source_target_pairs={{0,28},{4,0},{8,4},{12,8},{16,12},{20,16},{24,20},{28,24},{1,29},{... | collective-permute-start | bytes 786440 | tf_op jit(solution)/shard_map/ppermute | solution.py:43
  304.2 224.1 %all-gather.19.cloned.1.call-start = ((), (), s32[]{:S(2)}) async-start(), calls=%async_computation.5 | async-start | bytes 9502720 | tf_op jit(solution)/shard_map/all_gather | solution.py:58
  317.7 238.8 %all-gather.17.cloned.1.call-start = ((), (), s32[]{:S(2)}) async-start(), calls=%async_computation.4 | async-start | bytes 2359296 | tf_op jit(solution)/shard_map/all_gather | solution.py:52
  437.8 8.7 %collective-permute-start.14 = (bf16[128,1024]{1,0:T(8,128)(2,1)S(1)}, bf16[128,1024]{1,0:T(8,128)(2,1)S(1)}, u32[]{:S(2)}, u32[]{:S(2)}) collective-permute-start(bf16[128,1024]{1,0:T(8,128)(2,1)S(1)} %get-tuple-element.9), channel_id=1, source_target_pairs={{0,4},{4,8},{8,12},{12,16},{16,20},{20,24},{24,28},{28,0},{1,5},{5... | collective-permute-start | bytes 786440 | tf_op jit(solution)/shard_map/ppermute | solution.py:38
  438.1 8.4 %collective-permute-start.15 = (bf16[128,1024]{1,0:T(8,128)(2,1)S(1)}, bf16[128,1024]{1,0:T(8,128)(2,1)S(1)}, u32[]{:S(2)}, u32[]{:S(2)}) collective-permute-start(bf16[128,1024]{1,0:T(8,128)(2,1)S(1)} %get-tuple-element.9), channel_id=1, source_target_pairs={{0,28},{4,0},{8,4},{12,8},{16,12},{20,16},{24,20},{28,24},{1,29},{... | collective-permute-start | bytes 786440 | tf_op jit(solution)/shard_map/ppermute | solution.py:43
  446.5 9.2 %collective-permute-start.16 = (bf16[128,1024]{1,0:T(8,128)(2,1)S(1)}, bf16[128,1024]{1,0:T(8,128)(2,1)S(1)}, u32[]{:S(2)}, u32[]{:S(2)}) collective-permute-start(bf16[128,1024]{1,0:T(8,128)(2,1)S(1)} %collective-permute-done.14), channel_id=1, source_target_pairs={{0,4},{4,8},{8,12},{12,16},{16,20},{20,24},{24,28},{28,0},{1,5},{5... | collective-permute-start | bytes 786440 | tf_op jit(solution)/shard_map/ppermute | solution.py:38
  446.5 9.2 %collective-permute-start.17 = (bf16[128,1024]{1,0:T(8,128)(2,1)S(1)}, bf16[128,1024]{1,0:T(8,128)(2,1)S(1)}, u32[]{:S(2)}, u32[]{:S(2)}) collective-permute-start(bf16[128,1024]{1,0:T(8,128)(2,1)S(1)} %collective-permute-done.15), channel_id=1, source_target_pairs={{0,28},{4,0},{8,4},{12,8},{16,12},{20,16},{24,20},{28,24},{1,29},{... | collective-permute-start | bytes 786440 | tf_op jit(solution)/shard_map/ppermute | solution.py:43
  455.7 9.3 %collective-permute-start.18 = (bf16[128,1024]{1,0:T(8,128)(2,1)S(1)}, bf16[128,1024]{1,0:T(8,128)(2,1)S(1)}, u32[]{:S(2)}, u32[]{:S(2)}) collective-permute-start(bf16[128,1024]{1,0:T(8,128)(2,1)S(1)} %collective-permute-done.16), channel_id=1, source_target_pairs={{0,4},{4,8},{8,12},{12,16},{16,20},{20,24},{24,28},{28,0},{1,5},{5... | collective-permute-start | bytes 786440 | tf_op jit(solution)/shard_map/ppermute | solution.py:38
  455.8 9.3 %collective-permute-start.19 = (bf16[128,1024]{1,0:T(8,128)(2,1)S(1)}, bf16[128,1024]{1,0:T(8,128)(2,1)S(1)}, u32[]{:S(2)}, u32[]{:S(2)}) collective-permute-start(bf16[128,1024]{1,0:T(8,128)(2,1)S(1)} %collective-permute-done.17), channel_id=1, source_target_pairs={{0,28},{4,0},{8,4},{12,8},{16,12},{20,16},{24,20},{28,24},{1,29},{... | collective-permute-start | bytes 786440 | tf_op jit(solution)/shard_map/ppermute | solution.py:43
  473.5 217.2 %all-gather.23.cloned.1.call-start = ((), (), s32[]{:S(2)}) async-start(), calls=%async_computation.7 | async-start | bytes 9175040 | tf_op jit(solution)/shard_map/all_gather | solution.py:58
  482.8 236.2 %all-gather.21.cloned.1.call-start = ((), (), s32[]{:S(2)}) async-start(), calls=%async_computation.6 | async-start | bytes 2359296 | tf_op jit(solution)/shard_map/all_gather | solution.py:52
  603.6 8.8 %collective-permute-start.21 = (bf16[128,1024]{1,0:T(8,128)(2,1)S(1)}, bf16[128,1024]{1,0:T(8,128)(2,1)S(1)}, u32[]{:S(2)}, u32[]{:S(2)}) collective-permute-start(bf16[128,1024]{1,0:T(8,128)(2,1)S(1)} %get-tuple-element.7), channel_id=1, source_target_pairs={{0,4},{4,8},{8,12},{12,16},{16,20},{20,24},{24,28},{28,0},{1,5},{5... | collective-permute-start | bytes 786440 | tf_op jit(solution)/shard_map/ppermute | solution.py:38
  603.9 8.4 %collective-permute-start.22 = (bf16[128,1024]{1,0:T(8,128)(2,1)S(1)}, bf16[128,1024]{1,0:T(8,128)(2,1)S(1)}, u32[]{:S(2)}, u32[]{:S(2)}) collective-permute-start(bf16[128,1024]{1,0:T(8,128)(2,1)S(1)} %get-tuple-element.7), channel_id=1, source_target_pairs={{0,28},{4,0},{8,4},{12,8},{16,12},{20,16},{24,20},{28,24},{1,29},{... | collective-permute-start | bytes 786440 | tf_op jit(solution)/shard_map/ppermute | solution.py:43
  612.3 9.2 %collective-permute-start.23 = (bf16[128,1024]{1,0:T(8,128)(2,1)S(1)}, bf16[128,1024]{1,0:T(8,128)(2,1)S(1)}, u32[]{:S(2)}, u32[]{:S(2)}) collective-permute-start(bf16[128,1024]{1,0:T(8,128)(2,1)S(1)} %collective-permute-done.21), channel_id=1, source_target_pairs={{0,4},{4,8},{8,12},{12,16},{16,20},{20,24},{24,28},{28,0},{1,5},{5... | collective-permute-start | bytes 786440 | tf_op jit(solution)/shard_map/ppermute | solution.py:38
  612.3 9.3 %collective-permute-start.24 = (bf16[128,1024]{1,0:T(8,128)(2,1)S(1)}, bf16[128,1024]{1,0:T(8,128)(2,1)S(1)}, u32[]{:S(2)}, u32[]{:S(2)}) collective-permute-start(bf16[128,1024]{1,0:T(8,128)(2,1)S(1)} %collective-permute-done.22), channel_id=1, source_target_pairs={{0,28},{4,0},{8,4},{12,8},{16,12},{20,16},{24,20},{28,24},{1,29},{... | collective-permute-start | bytes 786440 | tf_op jit(solution)/shard_map/ppermute | solution.py:43
  621.5 9.3 %collective-permute-start.25 = (bf16[128,1024]{1,0:T(8,128)(2,1)S(1)}, bf16[128,1024]{1,0:T(8,128)(2,1)S(1)}, u32[]{:S(2)}, u32[]{:S(2)}) collective-permute-start(bf16[128,1024]{1,0:T(8,128)(2,1)S(1)} %collective-permute-done.23), channel_id=1, source_target_pairs={{0,4},{4,8},{8,12},{12,16},{16,20},{20,24},{24,28},{28,0},{1,5},{5... | collective-permute-start | bytes 786440 | tf_op jit(solution)/shard_map/ppermute | solution.py:38
  621.6 9.3 %collective-permute-start.26 = (bf16[128,1024]{1,0:T(8,128)(2,1)S(1)}, bf16[128,1024]{1,0:T(8,128)(2,1)S(1)}, u32[]{:S(2)}, u32[]{:S(2)}) collective-permute-start(bf16[128,1024]{1,0:T(8,128)(2,1)S(1)} %collective-permute-done.24), channel_id=1, source_target_pairs={{0,28},{4,0},{8,4},{12,8},{16,12},{20,16},{24,20},{28,24},{1,29},{... | collective-permute-start | bytes 786440 | tf_op jit(solution)/shard_map/ppermute | solution.py:43
  (8 other events, 74.3 us)
Sparse Core Ops, SparseCore 0:
  39.7 34.7 all-gather.8
  76.7 144.8 all-gather.10
  223.1 138.7 all-gather.14
  363.6 26.3 all-gather.12
  392.0 136.2 all-gather.18
  530.1 26.3 all-gather.16
  558.6 131.9 all-gather.22
  692.5 26.3 all-gather.20
